TPU v7x, 32 devices: a whole 2x2x4 slice. The times are simulated.
32 devices in a mesh: row: 8 (over y, x, core), col: 4 (over z).
Axes of the slice: x: 2, y: 2, z: 4, core: 2. Of those that a mesh axis runs over, the one named last changes fastest.
Arguments:
- pair: bfloat16 [256, 256, 128], P('row', 'col'), may hold values from -6 to 6
- cotangent: bfloat16 [256, 256, 128], P('row', 'col'), may hold values from -6 to 6
- length: int32 [1], replicated, may hold values from 128 to 256
- norm_gain: float32 [128], replicated, may hold values from 0.1 to 1.9
- norm_bias: float32 [128], replicated, may hold values from -1.5 to 1.5
- left_weight: bfloat16 [128, 256], replicated, may hold values from -0.5 to 0.5
- right_weight: bfloat16 [128, 256], replicated, may hold values from -0.5 to 0.5
- gate_weight: bfloat16 [128, 128], replicated, may hold values from -0.5 to 0.5
- out_gain: float32 [128], replicated, may hold values from 0.1 to 1.9
- out_bias: float32 [128], replicated, may hold values from -2 to 2
- out_weight: bfloat16 [128, 128], replicated, may hold values from -0.5 to 0.5
Outputs:
- update: bfloat16 [256, 256, 128], P('row', 'col')
- grad_pair: bfloat16 [256, 256, 128], P('row', 'col')
- grad_left: float32 [128, 256], replicated
- grad_right: float32 [128, 256], replicated
- grad_gating: float32 [128, 128], replicated
- grad_output: float32 [128, 128], replicated
- grad_norms: float32 [4, 128], replicated
Inputs may be any that keep to these rules, and one draw needn't show every extreme that they name: Tokens at positions 255 down to length are padding.
All inputs are finite; a program needn't handle non-finite values.
Results may differ from a plain program's by a relative error of at most 0.014.
Values may be sent and summed in bfloat16 or wider, within the bound.
No kernel may reach another device: no remote copies, remote signals or barrier semaphores. Data moves between devices by JAX's collectives and lax.ppermute only.
A program may use at most 128 MiB of HBM per device.

v0:
```python
import jax
import jax.numpy as jnp
from jax import lax
from jax.sharding import PartitionSpec as P

EPS = 1e-05


def broadcast(block, axis, holder):
    block = jnp.where(lax.axis_index(axis) == holder, block, jnp.zeros_like(block))
    return lax.psum(block, axis)


def normalize(values):
    center = values - jnp.mean(values, axis=-1, keepdims=True)
    inverse = lax.rsqrt(jnp.mean(center * center, axis=-1, keepdims=True) + EPS)
    return (center * inverse, inverse)


def gating(panel, weight, first_ok, second_ok, hidden):
    projected = jnp.einsum("ikc,ch->ikh", panel, weight, preferred_element_type=jnp.float32)
    values = projected[..., :hidden]
    sigmoid_val = jax.nn.sigmoid(projected[..., hidden:])
    pad_mask = (first_ok[:, None] & second_ok[None, :]).astype(jnp.float32)[..., None]
    return ((pad_mask * sigmoid_val * values).astype(jnp.bfloat16), values, sigmoid_val, pad_mask)


def push_back(partial_value, values, sigmoid_val, pad_mask, weight, panel):
    combined = jnp.concatenate(
        [
            partial_value * pad_mask * sigmoid_val,
            partial_value * pad_mask * values * sigmoid_val * (1.0 - sigmoid_val),
        ],
        axis=-1,
    ).astype(jnp.bfloat16)
    panel_grad = jnp.einsum("ikh,ch->ikc", combined, weight, preferred_element_type=jnp.float32)
    weight_grad = jnp.einsum("ikc,ikh->ch", panel, combined, preferred_element_type=jnp.float32)
    return (panel_grad, weight_grad)


def per_device(
    pair,
    cotangent,
    length,
    norm_gain,
    norm_bias,
    left_weight,
    right_weight,
    gate_weight,
    out_gain,
    out_bias,
    out_weight,
):
    row_index = lax.axis_index("row")
    col_index = lax.axis_index("col")
    n_row = lax.axis_size("row")
    n_col = lax.axis_size("col")
    per_col = n_row // n_col
    rows_dev = pair.shape[0]
    cols_dev = pair.shape[1]
    tokens = rows_dev * n_row
    hidden = out_weight.shape[0]
    pair_hat, pair_scale = normalize(pair.astype(jnp.float32))
    normed = (pair_hat * norm_gain + norm_bias).astype(jnp.bfloat16)
    real_count = length[0]
    second_ok = jnp.arange(tokens, dtype=jnp.int32) < real_count
    own_ok = row_index * rows_dev + jnp.arange(rows_dev, dtype=jnp.int32) < real_count
    partner_ok = col_index * cols_dev + jnp.arange(cols_dev, dtype=jnp.int32) < real_count
    left_tile, left_val, left_sig, tile_mask = gating(
        normed, left_weight, own_ok, partner_ok, hidden
    )
    right_tile, right_val, right_sig, unused_mask = gating(
        normed, right_weight, own_ok, partner_ok, hidden
    )
    row_panel = lax.all_gather(normed, "col", axis=1, tiled=True)
    pieces = []
    for member in range(per_col):
        pieces.append(broadcast(row_panel, "row", col_index * per_col + member))
    col_panel = jnp.concatenate(pieces, axis=0)
    left_act = gating(row_panel, left_weight, own_ok, second_ok, hidden)[0]
    right_act = gating(col_panel, right_weight, partner_ok, second_ok, hidden)[0]
    tri = jnp.einsum("ikh,jkh->ijh", left_act, right_act, preferred_element_type=jnp.float32)
    tri_hat, tri_scale = normalize(tri)
    tri_normed = (tri_hat * out_gain + out_bias).astype(jnp.bfloat16)
    outer_val = jnp.einsum(
        "ijh,hc->ijc", tri_normed, out_weight, preferred_element_type=jnp.float32
    )
    gate_val = jax.nn.sigmoid(
        jnp.einsum("ijc,cd->ijd", normed, gate_weight, preferred_element_type=jnp.float32)
    )
    update = (gate_val * outer_val).astype(jnp.bfloat16)
    upstream = cotangent.astype(jnp.float32)
    outer_grad = (upstream * gate_val).astype(jnp.bfloat16)
    gate_grad = (upstream * outer_val * gate_val * (1.0 - gate_val)).astype(jnp.bfloat16)
    grad_output = jnp.einsum(
        "ijh,ijc->hc", tri_normed, outer_grad, preferred_element_type=jnp.float32
    )
    grad_gating = jnp.einsum("ijc,ijd->cd", normed, gate_grad, preferred_element_type=jnp.float32)
    tnorm_grad = jnp.einsum(
        "ijc,hc->ijh", outer_grad, out_weight, preferred_element_type=jnp.float32
    )
    hat_grad = tnorm_grad * out_gain
    tri_grad = (
        tri_scale
        * (
            hat_grad
            - jnp.mean(hat_grad, axis=-1, keepdims=True)
            - tri_hat * jnp.mean(hat_grad * tri_hat, axis=-1, keepdims=True)
        )
    ).astype(jnp.bfloat16)
    row_partial = jnp.einsum(
        "ijh,jkh->ikh", tri_grad, right_act, preferred_element_type=jnp.float32
    )
    col_partial = jnp.einsum("ijh,ikh->jkh", tri_grad, left_act, preferred_element_type=jnp.float32)
    row_part = lax.psum_scatter(
        row_partial.astype(jnp.bfloat16), "col", scatter_dimension=1, tiled=True
    ).astype(jnp.float32)
    summed = lax.psum_scatter(
        col_partial.astype(jnp.bfloat16), "row", scatter_dimension=0, tiled=True
    )
    slab = summed[None]
    received = lax.all_to_all(slab, "col", split_axis=2, concat_axis=0, tiled=True)
    select = (jnp.arange(per_col, dtype=jnp.int32) == row_index // n_col).astype(jnp.bfloat16)
    spread = (received[:, None] * select[None, :, None, None, None]).reshape(
        (n_row,) + received.shape[1:]
    )
    returned = lax.all_to_all(spread, "row", split_axis=0, concat_axis=0, tiled=True)
    start = row_index % per_col * n_col
    owned = lax.dynamic_slice_in_dim(returned, start, n_col, 0).reshape(rows_dev, cols_dev, -1)
    col_part = owned.astype(jnp.float32)
    from_rows, grad_left = push_back(row_part, left_val, left_sig, tile_mask, left_weight, normed)
    from_cols, grad_right = push_back(
        col_part, right_val, right_sig, tile_mask, right_weight, normed
    )
    gate_back = jnp.einsum(
        "ijd,cd->ijc", gate_grad, gate_weight, preferred_element_type=jnp.float32
    )
    normed_grad = gate_back + from_rows + from_cols
    scaled = normed_grad * norm_gain
    grad_pair = (
        pair_scale
        * (
            scaled
            - jnp.mean(scaled, axis=-1, keepdims=True)
            - pair_hat * jnp.mean(scaled * pair_hat, axis=-1, keepdims=True)
        )
    ).astype(jnp.bfloat16)
    grad_norms = jnp.stack(
        [
            jnp.sum(normed_grad * pair_hat, axis=(0, 1)),
            jnp.sum(normed_grad, axis=(0, 1)),
            jnp.sum(tnorm_grad * tri_hat, axis=(0, 1)),
            jnp.sum(tnorm_grad, axis=(0, 1)),
        ]
    )
    totals = lax.psum((grad_left, grad_right, grad_gating, grad_output, grad_norms), ("row", "col"))
    inverse = 1.0 / tokens
    return (
        update,
        grad_pair,
        totals[0] * inverse,
        totals[1] * inverse,
        totals[2] * inverse,
        totals[3] * inverse,
        totals[4] * inverse,
    )


def solution(mesh):
    return jax.shard_map(
        per_device,
        mesh=mesh,
        in_specs=(
            P("row", "col", None),
            P("row", "col", None),
            P(),
            P(),
            P(),
            P(),
            P(),
            P(),
            P(),
            P(),
            P(),
        ),
        out_specs=(P("row", "col", None), P("row", "col", None), P(), P(), P(), P(), P()),
        check_vma=False,
    )
```

profile of v0, /device:TPU:0, one launch (start us, length us, event | category | flops | bytes accessed | tf_op | source)
XLA Modules:
  0.0 473.8 jit_solution(4896643660126480447)
XLA Ops:
  7.2 1.4 convert_reduce_fusion
  8.6 1.7 fusion.31
  10.3 2.5 fusion.25
  12.9 1.5 fusion.17
  14.4 47.0 %all-gather.2.cloned.1.call-done = bf16[32,256,128]{2,1,0:T(8,128)(2,1)} async-done(((bf16[32,64,128]{2,1,0:T(8,128)(2,1)}), bf16[32,256,128]{2,1,0:T(8,128)(2,1)}) %all-gather.2.cloned.1.call-update) | async-done | bytes 2097168 | tf_op jit(solution)/shard_map/all_gather | solution.py:75
  61.4 3.8 broadcast_select_fusion.1
  66.2 1.3 fusion.73
  68.3 3.1 copy.54
  71.5 2.8 fusion.53
  74.4 2.7 fusion.5
  77.0 4.6 copy.52
  81.6 63.4 %all-reduce.7.cloned.1.call-done = (bf16[32,256,128]{2,1,0:T(8,128)(2,1)}, bf16[32,256,128]{2,1,0:T(8,128)(2,1)}) async-done(((bf16[32,256,128]{2,1,0:T(8,128)(2,1)}, bf16[32,256,128]{2,1,0:T(8,128)(2,1)}), (bf16[32,256,128]{2,1,0:T(8,128)(2,1)}, bf16[32,256,128]{2,1,0:T(8,128)(2,1)})) %all-reduce.7.cloned.1.call-update) | async-done | bytes 4194320 | tf_op jit(solution)/shard_map/psum | solution.py:11
  145.1 4.5 fusion.10
  149.6 4.3 fusion
  154.0 6.8 %copy.51 = bf16[64,256,128]{1,0,2:T(8,128)(2,1)} copy(bf16[64,256,128]{2,1,0:T(8,128)(2,1)} %fusion) | data formatting | bytes 8388608 | tf_op jit(solution)/shard_map/convert_element_type | solution.py:25
  160.7 4.1 bitcast_reduce_fusion
  165.5 1.3 multiply_reduce_fusion
  166.8 1.8 multiply_convert_fusion
  168.6 1.3 fusion.74
  169.9 2.2 copy.66
  173.4 4.3 fusion.75
  177.7 4.6 copy.56
  182.5 41.1 %reduce-scatter.7.cloned.1.call-done = bf16[8,32768]{1,0:T(8,128)(2,1)} async-done(((bf16[64,32768]{1,0:T(8,128)(2,1)}), bf16[8,32768]{1,0:T(8,128)(2,1)}) %reduce-scatter.7.cloned.1.call-update) | async-done | bytes 524304
  223.6 1.2 copy.71
  225.1 1.3 copy.58
  226.4 4.6 all-to-all-start
  231.1 1.8 fusion.51
  232.9 1.7 fusion.56
  234.6 1.1 copy.53
  235.7 23.9 %all-to-all-done = bf16[1,8,256,128]{3,1,0,2:T(8,128)(2,1)} async-done(((bf16[1,8,256,128]{3,1,0,2:T(8,128)(2,1)}), bf16[1,8,256,128]{3,1,0,2:T(8,128)(2,1)}, u32[]{:S(2)}, u32[]{:S(2)}) %all-to-all-start) | async-done | bytes 524320 | tf_op jit(solution)/shard_map/all_to_all | solution.py:122
  259.6 1.2 copy.60
  260.8 1.1 bitcast_multiply_fusion
  261.9 4.2 all-to-all-start.1
  266.2 1.2 fusion.34
  269.7 11.9 %all-to-all-done.1 = bf16[8,8,64,128]{3,2,1,0:T(8,128)(2,1)} async-done(((bf16[8,8,64,128]{3,2,1,0:T(8,128)(2,1)}), bf16[8,8,64,128]{3,2,1,0:T(8,128)(2,1)}, u32[]{:S(2)}, u32[]{:S(2)}) %all-to-all-start.1) | async-done | bytes 1048608 | tf_op jit(solution)/shard_map/all_to_all | solution.py:127
  281.5 1.1 constant_dynamic-slice_fusion
  282.7 2.8 fusion.49
  285.5 1.0 convolution_bitcast_fusion.1
  286.5 1.4 convolution_add_fusion.1
  287.9 1.0 convolution_bitcast_fusion
  289.0 2.6 fusion.30
  291.6 37.2 %psum.55 = f32[4,128]{1,0:T(4,128)S(1)} all-reduce(f32[4,128]{1,0:T(4,128)S(1)} %pad_maximum_fusion.6), channel_id=1, replica_groups=mesh['row'=8,'col'=4] {'row','col'}, use_global_device_ids=true, to_apply=%region_20.21 | all-reduce | flops 512 | bytes 4096 | tf_op jit(solution)/shard_map/psum | solution.py:156
  328.8 1.9 fusion.29
  331.3 129.8 %all-reduce.5.cloned.1.call-done = (f32[128,256]{1,0:T(8,128)}, f32[128,256]{1,0:T(8,128)}, f32[128,128]{1,0:T(8,128)}, f32[128,128]{1,0:T(8,128)}) async-done(((f32[128,256]{1,0:T(8,128)}, f32[128,256]{1,0:T(8,128)}, f32[128,128]{1,0:T(8,128)}, f32[128,128]{1,0:T(8,128)}), (f32[128,256]{1,0:T(8,128)}, f32[128,256]{1,0:T(8,128)}, f32[128,128]{1,0:T(8,128)}, ...) | async-done | bytes 393232 | tf_op jit(solution)/shard_map/psum | solution.py:156
  461.2 1.6 broadcast_multiply_fusion
  462.7 1.6 broadcast_multiply_fusion.1
  464.3 1.5 broadcast_multiply_fusion.2
  465.8 1.5 broadcast_multiply_fusion.3
  (66 shorter events, 6.6 us)
Async XLA Ops:
  7.2 137.9 %copy-start = (bf16[128,256]{1,0:T(8,128)(2,1)S(1)}, bf16[128,256]{1,0:T(8,128)(2,1)}, u32[]{:S(2)}) copy-start(bf16[128,256]{1,0:T(8,128)(2,1)} %param.17) | copy-start | bytes 196612
  7.2 5.7 %copy-start.12 = (bf16[128,128]{1,0:T(8,128)(2,1)S(1)}, bf16[128,128]{1,0:T(8,128)(2,1)}, u32[]{:S(2)}) copy-start(bf16[128,128]{1,0:T(8,128)(2,1)} %param.18) | copy-start | bytes 98308
  7.2 54.2 %all-gather.2.cloned.1.call-start = ((), (), s32[]{:S(2)}) async-start(), calls=%async_computation.4 | async-start | bytes 2621440 | tf_op jit(solution)/shard_map/all_gather | solution.py:75
  12.8 132.2 %all-reduce.7.cloned.1.call-start = ((), (), s32[]{:S(2)}) async-start(), calls=%async_computation.8 | async-start | bytes 8388608 | tf_op jit(solution)/shard_map/psum | solution.py:11
  65.2 1.0 copy-start.6
  65.2 1.0 copy-start.11
  65.2 158.4 %reduce-scatter.7.cloned.1.call-start = ((), (), s32[]{:S(2)}) async-start(), calls=%async_computation.6 | async-start | bytes 4718592
  67.6 4.0 copy-start.9
  164.8 0.7 copy-start.14
  165.5 1.3 copy-start.15
  166.8 1.8 copy-start.1
  168.6 1.3 copy-start.3
  172.2 1.2 copy-start.4
  172.2 110.4 %reduce-scatter.5.cloned.1.call-start = ((), (), s32[]{:S(2)}) async-start(), calls=%async_computation.5 | async-start | bytes 2621440 | tf_op jit(solution)/shard_map/reduce_scatter | solution.py:115
  223.6 7.5 %copy-start.2 = (bf16[32,64,128]{2,1,0:T(8,128)(2,1)S(1)}, bf16[32,64,128]{2,1,0:T(8,128)(2,1)}, u32[]{:S(2)}) copy-start(bf16[32,64,128]{2,1,0:T(8,128)(2,1)} %fusion.25) | copy-start | bytes 1572868
  226.4 33.2 %all-to-all-start = ((bf16[1,8,256,128]{3,1,0,2:T(8,128)(2,1)}), bf16[1,8,256,128]{3,1,0,2:T(8,128)(2,1)}, u32[]{:S(2)}, u32[]{:S(2)}) async-start(bf16[1,8,256,128]{3,1,0,2:T(8,128)(2,1)} %copy.58), calls=%async_computation.1 | async-start | bytes 1048576 | tf_op jit(solution)/shard_map/all_to_all | solution.py:122
  231.1 3.5 copy-start.8
  260.8 5.4 %copy-start.7 = (bf16[32,64,128]{2,1,0:T(8,128)(2,1)S(1)}, bf16[32,64,128]{2,1,0:T(8,128)(2,1)}, u32[]{:S(2)}) copy-start(bf16[32,64,128]{2,1,0:T(8,128)(2,1)} %param.12) | copy-start | bytes 1572868
  261.9 19.6 %all-to-all-start.1 = ((bf16[8,8,64,128]{3,2,1,0:T(8,128)(2,1)}), bf16[8,8,64,128]{3,2,1,0:T(8,128)(2,1)}, u32[]{:S(2)}, u32[]{:S(2)}) async-start(bf16[8,8,64,128]{3,2,1,0:T(8,128)(2,1)} %bitcast_multiply_fusion), calls=%async_computation.2 | async-start | bytes 2097152 | tf_op jit(solution)/shard_map/all_to_all | solution.py:127
  266.2 195.0 %all-reduce.5.cloned.1.call-start = ((), (), s32[]{:S(2)}) async-start(), calls=%async_computation.7 | async-start | bytes 786432 | tf_op jit(solution)/shard_map/psum | solution.py:156
  285.5 2.5 copy-start.10
  286.5 2.5 copy-start.5
  286.5 2.5 copy-start.13
Sparse Core Ops, SparseCore 0:
  13.0 48.3 all-gather.1
  65.4 79.6 all-reduce.6
  172.3 51.2 reduce-scatter.6
  225.7 51.5 reduce-scatter.4
  330.9 130.2 all-reduce.4
where the time goes:
time: 475 us; the launch traced here: 474 us
  waiting for transfers between devices  317 us (67%)
  blocking collectives  37.2 us (8%)
  matrix products  32.8 us (7%)
  other arithmetic  32.6 us (7%)
  local copies, waits for them, and re-layouts  29.7 us (6%)
  between operations  14.8 us (3%)
  starting transfers between devices  9.43 us (2%)
    psum x1, waiting for transfers between devices, per_device(): lax.psum((grad_left, grad_right, grad_gating, grad_output, grad_norms), (...  130 us
    psum x1, waiting for transfers between devices, broadcast(): return lax.psum(block, axis)  63.4 us
    all_gather x1, waiting for transfers between devices, per_device(): row_panel = lax.all_gather(normed, 'col', axis=1, tiled=True)  47 us
    unnamed x6, waiting for transfers between devices  41.2 us
    psum x1, blocking collectives, per_device(): lax.psum((grad_left, grad_right, grad_gating, grad_output, grad_norms), (...  37.2 us
    all_to_all x1, waiting for transfers between devices, per_device(): lax.all_to_all(slab, 'col', split_axis=2, concat_axis=0, tiled=True)  23.9 us
    all_to_all x1, waiting for transfers between devices, per_device(): lax.all_to_all(spread, 'row', split_axis=0, concat_axis=0, tiled=True)  11.9 us
    convert_element_type x2, local copies, waits for them, and re-layouts, gating(): (pad_mask * sigmoid_val * values).astype(jnp.bfloat16)  11.4 us
  transfers between devices with their start and end apart: 7, of which 6 were waited for; matrix products, arithmetic and copies ran while one was open for 8% of the time, Pallas kernels for 0%

commit v1 on v0

--- a/solution.py
+++ b/solution.py
@@ -153,7 +153,9 @@
             jnp.sum(tnorm_grad, axis=(0, 1)),
         ]
     )
-    totals = lax.psum((grad_left, grad_right, grad_gating, grad_output, grad_norms), ("row", "col"))
+    totals = lax.psum(
+        lax.psum((grad_left, grad_right, grad_gating, grad_output, grad_norms), "col"), "row"
+    )
     inverse = 1.0 / tokens
     return (
         update,

time: 475 us -> 419 us (0.88)
  waiting for transfers between devices: 317 us -> 276 us
  blocking collectives: 37.2 us -> 22 us
    psum x1 -> x2, waiting for transfers between devices: 130 us -> 88.9 us  [the longest x1 57.5 us: per_device(): lax.psum(lax.psum((grad_left, grad_right, grad_gating, grad_output, grad_...]
    psum x1 -> x2, blocking collectives: 37.2 us -> 22 us  [the longest x1 11.8 us: per_device(): lax.psum(lax.psum((grad_left, grad_right, grad_gating, grad_output, grad_...]
    unnamed x6 -> x7, waiting for transfers between devices: 41.2 us -> 41.2 us
  transfers between devices with their start and end apart: 7 -> 8, of which waited for: 6 -> 7; matrix products, arithmetic and copies ran while one was open for 8% -> 10% of each run, Pallas kernels for 0% -> 0%
where the time goes in v1:
time: 419 us; the launch traced here: 418 us
  waiting for transfers between devices  276 us (66%)
  matrix products  32.8 us (8%)
  other arithmetic  32.6 us (8%)
  local copies, waits for them, and re-layouts  29.7 us (7%)
  blocking collectives  22 us (5%)
  between operations  15.1 us (4%)
  starting transfers between devices  9.47 us (2%)
    psum x1, waiting for transfers between devices, broadcast(): return lax.psum(block, axis)  63.4 us
    psum x1, waiting for transfers between devices, per_device(): lax.psum(lax.psum((grad_left, grad_right, grad_gating, grad_output, grad_...  57.5 us
    all_gather x1, waiting for transfers between devices, per_device(): row_panel = lax.all_gather(normed, 'col', axis=1, tiled=True)  47 us
    unnamed x7, waiting for transfers between devices  41.2 us
    psum x1, waiting for transfers between devices, per_device(): lax.psum((grad_left, grad_right, grad_gating, grad_output, grad_norms), '...  31.4 us
    all_to_all x1, waiting for transfers between devices, per_device(): lax.all_to_all(slab, 'col', split_axis=2, concat_axis=0, tiled=True)  23.9 us
    all_to_all x1, waiting for transfers between devices, per_device(): lax.all_to_all(spread, 'row', split_axis=0, concat_axis=0, tiled=True)  11.9 us
    psum x1, blocking collectives, per_device(): lax.psum(lax.psum((grad_left, grad_right, grad_gating, grad_output, grad_...  11.8 us
  transfers between devices with their start and end apart: 8, of which 7 were waited for; matrix products, arithmetic and copies ran while one was open for 10% of the time, Pallas kernels for 0%

profile of v1, /device:TPU:0, one launch (start us, length us, event | category | flops | bytes accessed | tf_op | source)
XLA Modules:
  0.0 418.1 jit_solution(16828417800669415097)
XLA Ops:
  7.2 1.4 convert_reduce_fusion
  8.6 1.7 fusion.31
  10.3 2.5 fusion.25
  12.9 1.5 fusion.17
  14.4 47.0 %all-gather.2.cloned.1.call-done = bf16[32,256,128]{2,1,0:T(8,128)(2,1)} async-done(((bf16[32,64,128]{2,1,0:T(8,128)(2,1)}), bf16[32,256,128]{2,1,0:T(8,128)(2,1)}) %all-gather.2.cloned.1.call-update) | async-done | bytes 2097168 | tf_op jit(solution)/shard_map/all_gather | solution.py:75
  61.4 3.8 broadcast_select_fusion.1
  66.2 1.3 fusion.73
  68.3 3.1 copy.54
  71.5 2.8 fusion.53
  74.4 2.7 fusion.5
  77.0 4.6 %copy.52 = bf16[32,256,128]{1,0,2:T(8,128)(2,1)} copy(bf16[32,256,128]{2,1,0:T(8,128)(2,1)} %fusion.5) | data formatting | bytes 4194304 | tf_op jit(solution)/shard_map/convert_element_type | solution.py:25
  81.6 63.4 %all-reduce.11.cloned.1.call-done = (bf16[32,256,128]{2,1,0:T(8,128)(2,1)}, bf16[32,256,128]{2,1,0:T(8,128)(2,1)}) async-done(((bf16[32,256,128]{2,1,0:T(8,128)(2,1)}, bf16[32,256,128]{2,1,0:T(8,128)(2,1)}), (bf16[32,256,128]{2,1,0:T(8,128)(2,1)}, bf16[32,256,128]{2,1,0:T(8,128)(2,1)})) %all-reduce.11.cloned.1.call-update) | async-done | bytes 4194320 | tf_op jit(solution)/shard_map/psum | solution.py:11
  145.1 4.5 %fusion.10 = f32[64,256,256]{2,1,0:T(8,128)S(1)} fusion(bf16[32,256,128]{2,1,0:T(8,128)(2,1)} %get-tuple-element.22, bf16[32,256,128]{2,1,0:T(8,128)(2,1)} %get-tuple-element.23, bf16[128,256]{1,0:T(8,128)(2,1)S(1)} %copy-done), kind=kOutput, calls=%fused_computation.14 | convolution fusion | flops 1075838976 | bytes 21037056 | tf_op jit(solution)/shard_map/ikc,ch->ikh/dot_general | solution.py:21
  149.6 4.3 %fusion = bf16[64,256,128]{2,1,0:T(8,128)(2,1)} fusion(f32[64,256,256]{2,1,0:T(8,128)S(1)} %fusion.10, f32[64,256]{1,0:T(8,128)S(1)} %and_convert_fusion), kind=kLoop, calls=%fused_computation.1 | loop fusion | flops 12582912 | bytes 21037056 | tf_op jit(solution)/shard_map/convert_element_type | solution.py:25
  154.0 6.8 %copy.51 = bf16[64,256,128]{1,0,2:T(8,128)(2,1)} copy(bf16[64,256,128]{2,1,0:T(8,128)(2,1)} %fusion) | data formatting | bytes 8388608 | tf_op jit(solution)/shard_map/convert_element_type | solution.py:25
  160.7 4.1 bitcast_reduce_fusion
  165.5 1.3 multiply_reduce_fusion
  166.8 1.8 multiply_convert_fusion
  168.6 1.3 fusion.74
  169.9 2.2 copy.66
  173.4 4.3 %fusion.75 = bf16[128,256,32]{1,2,0:T(8,128)(2,1)} fusion(bf16[32,64,128]{1,0,2:T(8,128)(2,1)S(1)} %copy-done.4, bf16[64,256,128]{1,0,2:T(8,128)(2,1)} %copy.51), kind=kOutput, calls=%fused_computation.136 | convolution fusion | flops 134217728 | bytes 6815744 | tf_op jit(solution)/shard_map/ijh,jkh->ikh/dot_general | solution.py:111
  177.7 4.6 %copy.56 = bf16[128,256,32]{0,1,2:T(8,128)(2,1)} copy(bf16[128,256,32]{1,2,0:T(8,128)(2,1)} %fusion.75) | data formatting | bytes 4194304 | tf_op jit(solution)/shard_map/ijh,jkh->ikh/dot_general | solution.py:111
  182.5 41.1 %reduce-scatter.7.cloned.1.call-done = bf16[8,32768]{1,0:T(8,128)(2,1)} async-done(((bf16[64,32768]{1,0:T(8,128)(2,1)}), bf16[8,32768]{1,0:T(8,128)(2,1)}) %reduce-scatter.7.cloned.1.call-update) | async-done | bytes 524304
  223.6 1.2 copy.71
  225.1 1.3 copy.58
  226.4 4.6 %all-to-all-start = ((bf16[1,8,256,128]{3,1,0,2:T(8,128)(2,1)}), bf16[1,8,256,128]{3,1,0,2:T(8,128)(2,1)}, u32[]{:S(2)}, u32[]{:S(2)}) async-start(bf16[1,8,256,128]{3,1,0,2:T(8,128)(2,1)} %copy.58), calls=%async_computation.1 | async-start | bytes 1048576 | tf_op jit(solution)/shard_map/all_to_all | solution.py:122
  231.1 1.8 fusion.51
  232.9 1.7 fusion.56
  234.6 1.1 copy.53
  235.7 23.9 %all-to-all-done = bf16[1,8,256,128]{3,1,0,2:T(8,128)(2,1)} async-done(((bf16[1,8,256,128]{3,1,0,2:T(8,128)(2,1)}), bf16[1,8,256,128]{3,1,0,2:T(8,128)(2,1)}, u32[]{:S(2)}, u32[]{:S(2)}) %all-to-all-start) | async-done | bytes 524320 | tf_op jit(solution)/shard_map/all_to_all | solution.py:122
  259.6 1.2 copy.60
  260.8 1.1 bitcast_multiply_fusion
  261.9 4.2 %all-to-all-start.1 = ((bf16[8,8,64,128]{3,2,1,0:T(8,128)(2,1)}), bf16[8,8,64,128]{3,2,1,0:T(8,128)(2,1)}, u32[]{:S(2)}, u32[]{:S(2)}) async-start(bf16[8,8,64,128]{3,2,1,0:T(8,128)(2,1)} %bitcast_multiply_fusion), calls=%async_computation.2 | async-start | bytes 2097152 | tf_op jit(solution)/shard_map/all_to_all | solution.py:127
  266.2 1.2 fusion.34
  269.7 11.9 %all-to-all-done.1 = bf16[8,8,64,128]{3,2,1,0:T(8,128)(2,1)} async-done(((bf16[8,8,64,128]{3,2,1,0:T(8,128)(2,1)}), bf16[8,8,64,128]{3,2,1,0:T(8,128)(2,1)}, u32[]{:S(2)}, u32[]{:S(2)}) %all-to-all-start.1) | async-done | bytes 1048608 | tf_op jit(solution)/shard_map/all_to_all | solution.py:127
  281.5 1.1 constant_dynamic-slice_fusion
  282.7 2.8 fusion.49
  286.5 1.4 convolution_add_fusion.1
  289.0 2.6 fusion.30
  291.6 10.3 %psum.94 = f32[4,128]{1,0:T(4,128)S(1)} all-reduce(f32[4,128]{1,0:T(4,128)S(1)} %pad_maximum_fusion.6), channel_id=1, replica_groups=mesh['row'=8,'col'=4] {'col'}, use_global_device_ids=true, to_apply=%region_24.25 | all-reduce | flops 512 | bytes 4096 | tf_op jit(solution)/shard_map/psum | solution.py:157
  301.8 11.8 %psum.95 = f32[4,128]{1,0:T(4,128)S(1)} all-reduce(f32[4,128]{1,0:T(4,128)S(1)} %psum.94), channel_id=1, replica_groups=mesh['row'=8,'col'=4] {'row'}, use_global_device_ids=true, to_apply=%region_25.26 | all-reduce | flops 512 | bytes 4096 | tf_op jit(solution)/shard_map/psum | solution.py:156
  313.7 2.0 fusion.29
  315.7 31.4 %all-reduce.9.cloned.1.call-done = (f32[128,256]{1,0:T(8,128)}, f32[128,256]{1,0:T(8,128)}, f32[128,128]{1,0:T(8,128)}, f32[128,128]{1,0:T(8,128)}) async-done(((f32[128,256]{1,0:T(8,128)}, f32[128,256]{1,0:T(8,128)}, f32[128,128]{1,0:T(8,128)}, f32[128,128]{1,0:T(8,128)}), (f32[128,256]{1,0:T(8,128)}, f32[128,256]{1,0:T(8,128)}, f32[128,128]{1,0:T(8,128)}, ...) | async-done | bytes 393232 | tf_op jit(solution)/shard_map/psum | solution.py:157
  347.6 57.5 %all-reduce.7.cloned.1.call-done = (f32[128,256]{1,0:T(8,128)}, f32[128,256]{1,0:T(8,128)}, f32[128,128]{1,0:T(8,128)}, f32[128,128]{1,0:T(8,128)}) async-done(((f32[128,256]{1,0:T(8,128)}, f32[128,256]{1,0:T(8,128)}, f32[128,128]{1,0:T(8,128)}, f32[128,128]{1,0:T(8,128)}), (f32[128,256]{1,0:T(8,128)}, f32[128,256]{1,0:T(8,128)}, f32[128,128]{1,0:T(8,128)}, ...) | async-done | bytes 393232 | tf_op jit(solution)/shard_map/psum | solution.py:156
  405.1 1.6 broadcast_multiply_fusion
  406.7 1.6 broadcast_multiply_fusion.1
  408.3 1.5 broadcast_multiply_fusion.2
  409.7 1.5 broadcast_multiply_fusion.3
  (70 shorter events, 8.7 us)
Async XLA Ops:
  7.2 137.9 %copy-start = (bf16[128,256]{1,0:T(8,128)(2,1)S(1)}, bf16[128,256]{1,0:T(8,128)(2,1)}, u32[]{:S(2)}) copy-start(bf16[128,256]{1,0:T(8,128)(2,1)} %param.17) | copy-start | bytes 196612
  7.2 5.7 %copy-start.12 = (bf16[128,128]{1,0:T(8,128)(2,1)S(1)}, bf16[128,128]{1,0:T(8,128)(2,1)}, u32[]{:S(2)}) copy-start(bf16[128,128]{1,0:T(8,128)(2,1)} %param.18) | copy-start | bytes 98308
  7.2 54.2 %all-gather.2.cloned.1.call-start = ((), (), s32[]{:S(2)}) async-start(), calls=%async_computation.4 | async-start | bytes 2621440 | tf_op jit(solution)/shard_map/all_gather | solution.py:75
  12.8 132.2 %all-reduce.11.cloned.1.call-start = ((), (), s32[]{:S(2)}) async-start(), calls=%async_computation.9 | async-start | bytes 8388608 | tf_op jit(solution)/shard_map/psum | solution.py:11
  65.2 1.0 copy-start.6
  65.2 1.0 copy-start.11
  65.2 158.4 %reduce-scatter.7.cloned.1.call-start = ((), (), s32[]{:S(2)}) async-start(), calls=%async_computation.6 | async-start | bytes 4718592
  67.6 4.0 copy-start.9
  164.8 0.7 copy-start.14
  165.5 1.3 copy-start.15
  166.8 1.8 copy-start.1
  168.6 1.3 copy-start.3
  172.2 1.2 copy-start.4
  172.2 110.4 %reduce-scatter.5.cloned.1.call-start = ((), (), s32[]{:S(2)}) async-start(), calls=%async_computation.5 | async-start | bytes 2621440 | tf_op jit(solution)/shard_map/reduce_scatter | solution.py:115
  223.6 7.5 %copy-start.2 = (bf16[32,64,128]{2,1,0:T(8,128)(2,1)S(1)}, bf16[32,64,128]{2,1,0:T(8,128)(2,1)}, u32[]{:S(2)}) copy-start(bf16[32,64,128]{2,1,0:T(8,128)(2,1)} %fusion.25) | copy-start | bytes 1572868
  226.4 33.2 %all-to-all-start = ((bf16[1,8,256,128]{3,1,0,2:T(8,128)(2,1)}), bf16[1,8,256,128]{3,1,0,2:T(8,128)(2,1)}, u32[]{:S(2)}, u32[]{:S(2)}) async-start(bf16[1,8,256,128]{3,1,0,2:T(8,128)(2,1)} %copy.58), calls=%async_computation.1 | async-start | bytes 1048576 | tf_op jit(solution)/shard_map/all_to_all | solution.py:122
  231.1 3.5 copy-start.8
  260.8 5.4 %copy-start.7 = (bf16[32,64,128]{2,1,0:T(8,128)(2,1)S(1)}, bf16[32,64,128]{2,1,0:T(8,128)(2,1)}, u32[]{:S(2)}) copy-start(bf16[32,64,128]{2,1,0:T(8,128)(2,1)} %param.12) | copy-start | bytes 1572868
  261.9 19.6 %all-to-all-start.1 = ((bf16[8,8,64,128]{3,2,1,0:T(8,128)(2,1)}), bf16[8,8,64,128]{3,2,1,0:T(8,128)(2,1)}, u32[]{:S(2)}, u32[]{:S(2)}) async-start(bf16[8,8,64,128]{3,2,1,0:T(8,128)(2,1)} %bitcast_multiply_fusion), calls=%async_computation.2 | async-start | bytes 2097152 | tf_op jit(solution)/shard_map/all_to_all | solution.py:127
  266.2 80.9 %all-reduce.9.cloned.1.call-start = ((), (), s32[]{:S(2)}) async-start(), calls=%async_computation.8 | async-start | bytes 786432 | tf_op jit(solution)/shard_map/psum | solution.py:157
  285.5 2.5 copy-start.10
  286.5 2.5 copy-start.5
  286.5 2.5 copy-start.13
  313.6 91.5 %all-reduce.7.cloned.1.call-start = ((), (), s32[]{:S(2)}) async-start(), calls=%async_computation.7 | async-start | bytes 786432 | tf_op jit(solution)/shard_map/psum | solution.py:156
Sparse Core Ops, SparseCore 0:
  13.0 48.3 all-gather.1
  65.4 79.6 all-reduce.10
  172.3 51.2 reduce-scatter.6
  225.7 51.5 reduce-scatter.4
  313.8 33.2 all-reduce.8
  350.3 54.7 all-reduce.6
